TPU v7x, 128 devices: a whole 4x4x4 slice. The times are simulated.
128 devices in a mesh: dp: 4 (over z), context: 4 (over y), tensor: 8 (over x, core).
Axes of the slice: x: 4, y: 4, z: 4, core: 2. Of those that a mesh axis runs over, the one named last changes fastest.
Arguments:
- inputs: bfloat16 [8192, 5376], P(('dp', 'context')), may hold values from -8 to 8
- queries: bfloat16 [8192, 2048], P(('dp', 'context'), 'tensor'), may hold values from -8 to 8
- key_states: bfloat16 [8192, 1024], P(('dp', 'context'), 'tensor'), may hold values from -8 to 8
- value_states: bfloat16 [8192, 1024], P(('dp', 'context'), 'tensor'), may hold values from -6 to 6
- out_grad: bfloat16 [8192, 5376], P(('dp', 'context')), may hold values from -8 to 8
- positions: int32 [8192], P(('dp', 'context')), may hold values from 0 to 10239, as said below
- w_query: bfloat16 [5376, 2048], P(None, 'tensor'), may hold values from -0.078125 to 0.078125
- w_key: bfloat16 [5376, 1024], P(None, 'tensor'), may hold values from -0.078125 to 0.078125
- w_value: bfloat16 [5376, 1024], P(None, 'tensor'), may hold values from -0.078125 to 0.078125
- w_output: bfloat16 [5376, 2048], P(None, 'tensor'), may hold values from -0.125 to 0.125
Outputs:
- input_grad: bfloat16 [8192, 5376], P(('dp', 'context', 'tensor'))
- grad_query: float32 [5376, 2048], P(('dp', 'context'), 'tensor')
- grad_key: float32 [5376, 1024], P(('dp', 'context'), 'tensor')
- grad_value: float32 [5376, 1024], P(('dp', 'context'), 'tensor')
- grad_output: float32 [5376, 2048], P(('dp', 'context'), 'tensor')
Inputs may be any that keep to these rules, and one draw needn't show every extreme that they name: Within a document positions rise by one from token to token; a position of 0 starts a new document; the first document of each replica's 2048 tokens may have begun before them.
All inputs are finite; a program needn't handle non-finite values.
Results may differ from a plain program's by a relative error of at most 0.02.
Values may be sent and summed in bfloat16 or wider, within the bound.
A program may use at most 128 MiB of HBM per device.

v0:
```python
import jax
import jax.numpy as jnp
from jax import lax
from jax.sharding import PartitionSpec as P

HD = 128
W = 1024
QSCALAR = 168


def rotate_back(grads, places):
    count = grads.shape[0]
    half = HD // 2
    index = jnp.arange(half, dtype=jnp.float32)
    freq = jnp.power(jnp.float32(10000.0), index * (-2.0 / HD))
    angle = places.astype(jnp.float32)[:, None] * freq[None, :]
    cosine = jnp.cos(angle)[:, None, :]
    sine = jnp.sin(angle)[:, None, :]
    split = grads.reshape(count, -1, 2, half)
    first = split[:, :, 0, :]
    second = split[:, :, 1, :]
    upper = first * cosine + second * sine
    lower = second * cosine - first * sine
    return jnp.stack([upper, lower], axis=2).reshape(count, -1)


def contract_rows(left, right):
    return lax.dot_general(
        left, right, (((0,), (0,)), ((), ())), preferred_element_type=jnp.float32
    )


def contract_cols(left, right):
    return lax.dot_general(
        left, right, (((1,), (1,)), ((), ())), preferred_element_type=jnp.float32
    )


def on_device(
    inputs,
    queries,
    key_states,
    value_states,
    out_grad,
    positions,
    w_query,
    w_key,
    w_value,
    w_output,
):
    count = queries.shape[0]
    head_cols = queries.shape[1]
    kv_cols = key_states.shape[1]
    kv_here = kv_cols // HD
    group = head_cols // kv_cols
    scale = QSCALAR ** (-0.5)
    block = lax.axis_index("context")
    blocks = lax.axis_size("context")
    reach = min((W + count - 2) // count, blocks - 1)
    span = (reach + 1) * count
    whole_keys, whole_values = (
        lax.all_gather(key_states, "context", axis=0, tiled=True),
        lax.all_gather(value_states, "context", axis=0, tiled=True),
    )
    padding = jnp.zeros((reach * count, kv_cols), jnp.bfloat16)
    band_keys = lax.dynamic_slice_in_dim(
        jnp.concatenate([padding, whole_keys], axis=0), block * count, span, 0
    )
    band_values = lax.dynamic_slice_in_dim(
        jnp.concatenate([padding, whole_values], axis=0), block * count, span, 0
    )
    query_index = block * count + jnp.arange(count, dtype=jnp.int32)
    key_index = (block - reach) * count + jnp.arange(span, dtype=jnp.int32)
    doc_start = query_index - positions
    allowed = (key_index[None, :] <= query_index[:, None]) & (
        query_index[:, None] - key_index[None, :] < W
    )
    allowed = allowed & (key_index[None, :] >= doc_start[:, None]) & (key_index[None, :] >= 0)
    query_heads = queries.reshape(count, kv_here, group, HD)
    key_heads = band_keys.reshape(span, kv_here, HD)
    value_heads = band_values.reshape(span, kv_here, HD)
    scores = (
        jnp.einsum("qhgd,khd->hgqk", query_heads, key_heads, preferred_element_type=jnp.float32)
        * scale
    )
    scores = jnp.where(allowed, scores, -1e30)
    top = jnp.max(scores, axis=-1, keepdims=True)
    weights = jnp.exp(scores - top)
    probs = weights / jnp.sum(weights, axis=-1, keepdims=True)
    probs_half = probs.astype(jnp.bfloat16)
    attn = jnp.einsum(
        "hgqk,khd->qhgd", probs_half, value_heads, preferred_element_type=jnp.float32
    ).astype(jnp.bfloat16)
    attn_flat = attn.reshape(count, head_cols)
    dattn = jnp.dot(out_grad, w_output, preferred_element_type=jnp.float32).astype(jnp.bfloat16)
    dattn_heads = dattn.reshape(count, kv_here, group, HD)
    dprobs = jnp.einsum(
        "qhgd,khd->hgqk", dattn_heads, value_heads, preferred_element_type=jnp.float32
    )
    delta = jnp.sum(dattn_heads.astype(jnp.float32) * attn.astype(jnp.float32), axis=-1)
    delta = jnp.transpose(delta, (1, 2, 0))[..., None]
    dscores = (probs * (dprobs - delta) * scale).astype(jnp.bfloat16)
    query_grad = jnp.einsum(
        "hgqk,khd->qhgd", dscores, key_heads, preferred_element_type=jnp.float32
    ).reshape(count, head_cols)
    band_key_grad = jnp.einsum(
        "hgqk,qhgd->khd", dscores, query_heads, preferred_element_type=jnp.float32
    ).reshape(span, kv_cols)
    band_value_grad = jnp.einsum(
        "hgqk,qhgd->khd", probs_half, dattn_heads, preferred_element_type=jnp.float32
    ).reshape(span, kv_cols)
    seg_len = blocks * count
    empty = jnp.zeros((seg_len + reach * count, kv_cols), jnp.float32)
    full_keys = lax.dynamic_update_slice_in_dim(empty, band_key_grad, block * count, 0)[
        reach * count :
    ]
    full_values = lax.dynamic_update_slice_in_dim(empty, band_value_grad, block * count, 0)[
        reach * count :
    ]
    key_grad, value_grad = (
        lax.psum_scatter(full_keys, "context", scatter_dimension=0, tiled=True),
        lax.psum_scatter(full_values, "context", scatter_dimension=0, tiled=True),
    )
    query_lin = rotate_back(query_grad, positions).astype(jnp.bfloat16)
    key_lin = rotate_back(key_grad, positions).astype(jnp.bfloat16)
    value_half = value_grad.astype(jnp.bfloat16)
    total = contract_cols(query_lin, w_query)
    total = total + contract_cols(key_lin, w_key)
    total = total + contract_cols(value_half, w_value)
    input_grad = lax.psum_scatter(total, "tensor", scatter_dimension=0, tiled=True).astype(
        jnp.bfloat16
    )
    terms = (
        contract_rows(inputs, query_lin),
        contract_rows(inputs, key_lin),
        contract_rows(inputs, value_half),
        contract_rows(out_grad, attn_flat),
    )
    summed = (
        lax.psum_scatter(
            terms[0].astype(jnp.bfloat16), ("dp", "context"), scatter_dimension=0, tiled=True
        ).astype(jnp.float32),
        lax.psum_scatter(
            terms[1].astype(jnp.bfloat16), ("dp", "context"), scatter_dimension=0, tiled=True
        ).astype(jnp.float32),
        lax.psum_scatter(
            terms[2].astype(jnp.bfloat16), ("dp", "context"), scatter_dimension=0, tiled=True
        ).astype(jnp.float32),
        lax.psum_scatter(
            terms[3].astype(jnp.bfloat16), ("dp", "context"), scatter_dimension=0, tiled=True
        ).astype(jnp.float32),
    )
    return (input_grad, summed[0], summed[1], summed[2], summed[3])


def solution(mesh):
    return jax.shard_map(
        on_device,
        mesh=mesh,
        in_specs=(
            P(("dp", "context"), None),
            P(("dp", "context"), "tensor"),
            P(("dp", "context"), "tensor"),
            P(("dp", "context"), "tensor"),
            P(("dp", "context"), None),
            P(("dp", "context")),
            P(None, "tensor"),
            P(None, "tensor"),
            P(None, "tensor"),
            P(None, "tensor"),
        ),
        out_specs=(
            P(("dp", "context", "tensor"), None),
            P(("dp", "context"), "tensor"),
            P(("dp", "context"), "tensor"),
            P(("dp", "context"), "tensor"),
            P(("dp", "context"), "tensor"),
        ),
        check_vma=False,
    )
```

profile of v0, /device:TPU:1, one launch (start us, length us, event | category | flops | bytes accessed | tf_op | source)
XLA Modules:
  0.0 441.3 jit_solution(8427026727097141793)
XLA Ops:
  9.3 13.3 %all_gather.6 = bf16[2048,128]{1,0:T(8,128)(2,1)} all-gather(bf16[512,128]{1,0:T(8,128)(2,1)} %param.12), channel_id=1, replica_groups=mesh['dp'=4,'context'=4,'tensor'=8] {'context'}, dimensions={0}, use_global_device_ids=true | all-gather | bytes 655360 | tf_op jit(solution)/shard_map/all_gather | solution.py:62
  22.6 10.8 %all_gather.7 = bf16[2048,128]{1,0:T(8,128)(2,1)} all-gather(bf16[512,128]{1,0:T(8,128)(2,1)} %param.13), channel_id=1, replica_groups=mesh['dp'=4,'context'=4,'tensor'=8] {'context'}, dimensions={0}, use_global_device_ids=true | all-gather | bytes 655360 | tf_op jit(solution)/shard_map/all_gather | solution.py:63
  33.4 2.3 fusion.17
  35.7 2.5 fusion.9
  39.8 2.3 copy-done.8
  43.7 3.1 fusion.29
  46.8 3.2 fusion.10
  54.2 4.2 fusion.22
  59.8 23.1 %reduce-scatter.12.cloned.1.call-done = f32[512,128]{0,1:T(8,128)} async-done(((f32[2048,128]{0,1:T(8,128)}), f32[512,128]{0,1:T(8,128)}) %reduce-scatter.12.cloned.1.call-update) | async-done | bytes 262160 | tf_op jit(solution)/shard_map/reduce_scatter | solution.py:121
  84.4 4.6 %fusion.2 = bf16[5376,128]{0,1:T(8,128)(2,1)} fusion(bf16[512,128]{0,1:T(8,128)(2,1)S(1)} %bitcast.146, bf16[512,5376]{1,0:T(8,128)(2,1)} %param.10), kind=kOutput, calls=%fused_computation.7 | convolution fusion | flops 705331200 | bytes 7012352 | tf_op jit(solution)/shard_map/dot_general | solution.py:28
  89.0 19.8 %reduce-scatter.14.cloned.1.call-done = f32[512,128]{0,1:T(8,128)} async-done(((f32[2048,128]{0,1:T(8,128)}), f32[512,128]{0,1:T(8,128)}) %reduce-scatter.14.cloned.1.call-update) | async-done | bytes 262160 | tf_op jit(solution)/shard_map/reduce_scatter | solution.py:122
  108.8 4.6 %fusion.3 = bf16[5376,128]{0,1:T(8,128)(2,1)} fusion(bf16[512,5376]{1,0:T(8,128)(2,1)} %param.10, f32[512,128]{0,1:T(8,128)} %reduce-scatter.14.cloned.1.call-done), kind=kOutput, calls=%fused_computation.8 | convolution fusion | flops 705396736 | bytes 7143424 | tf_op jit(solution)/shard_map/dot_general | solution.py:28
  114.1 2.8 fusion.36
  117.0 5.7 %fusion = bf16[5376,256]{0,1:T(8,128)(2,1)} fusion(bf16[512,256]{0,1:T(8,128)(2,1)S(1)} %bitcast.148, bf16[512,5376]{1,0:T(8,128)(2,1)} %param.10), kind=kOutput, calls=%fused_computation.3 | convolution fusion | flops 1410662400 | bytes 8519680 | tf_op jit(solution)/shard_map/dot_general | solution.py:28
  122.7 4.8 %copy.64 = bf16[5376,256]{1,0:T(8,128)(2,1)} copy(bf16[5376,256]{0,1:T(8,128)(2,1)} %fusion) | data formatting | bytes 5505024
  127.7 5.8 %fusion.1 = bf16[5376,256]{0,1:T(8,128)(2,1)} fusion(bf16[512,256]{0,1:T(8,128)(2,1)S(1)} %bitcast.153, bf16[512,5376]{1,0:T(8,128)(2,1)} %param.14), kind=kOutput, calls=%fused_computation.4 | convolution fusion | flops 1410662400 | bytes 8519680 | tf_op jit(solution)/shard_map/dot_general | solution.py:28
  133.5 4.7 %copy.70 = bf16[5376,256]{1,0:T(8,128)(2,1)} copy(bf16[5376,256]{0,1:T(8,128)(2,1)} %fusion.1) | data formatting | bytes 5505024
  138.5 3.1 fusion.65
  141.6 5.8 %fusion.51 = f32[512,5376]{1,0:T(8,128)} fusion(bf16[5376,128]{1,0:T(8,128)(2,1)S(1)} %copy-done.4, f32[512,128]{0,1:T(8,128)S(1)} %copy-done.5), kind=kOutput, calls=%fused_computation.65 | convolution fusion | flops 704708608 | bytes 12648448 | tf_op jit(solution)/shard_map/dot_general | solution.py:34
  147.4 10.0 %add_add_fusion = f32[512,5376]{1,0:T(8,128)} fusion(f32[512,5376]{1,0:T(8,128)} %fusion.51, f32[512,5376]{1,0:T(8,128)S(1)} %fusion.65, bf16[512,256]{0,1:T(8,128)(2,1)S(1)} %bitcast.149, bf16[5376,256]{1,0:T(8,128)(2,1)S(1)} %copy-done), kind=kOutput, calls=%fused_computation | convolution fusion | flops 1414791168 | bytes 36044800 | tf_op jit(solution)/shard_map/dot_general | solution.py:34
  159.3 49.0 %all-reduce.7.cloned.1.call-done = (bf16[5376,128]{0,1:T(8,128)(2,1)}, bf16[5376,128]{0,1:T(8,128)(2,1)}) async-done(((bf16[5376,128]{0,1:T(8,128)(2,1)}, bf16[5376,128]{0,1:T(8,128)(2,1)}), (bf16[5376,128]{0,1:T(8,128)(2,1)}, bf16[5376,128]{0,1:T(8,128)(2,1)})) %all-reduce.7.cloned.1.call-update) | async-done | bytes 2752528
  211.0 74.9 %reduce-scatter.18.cloned.1.call-done = bf16[336,256]{1,0:T(8,128)(2,1)} async-done(((bf16[5376,256]{1,0:T(8,128)(2,1)}), bf16[336,256]{1,0:T(8,128)(2,1)}) %reduce-scatter.18.cloned.1.call-update) | async-done | bytes 172048
  287.8 76.9 %reduce-scatter.20.cloned.1.call-done = bf16[336,256]{1,0:T(8,128)(2,1)} async-done(((bf16[5376,256]{1,0:T(8,128)(2,1)}), bf16[336,256]{1,0:T(8,128)(2,1)}) %reduce-scatter.20.cloned.1.call-update) | async-done | bytes 172048
  366.7 65.5 %reduce-scatter.16.cloned.1.call-done = f32[64,5376]{1,0:T(8,128)} async-done(((f32[512,5376]{1,0:T(8,128)}), f32[64,5376]{1,0:T(8,128)}) %reduce-scatter.16.cloned.1.call-update) | async-done | bytes 1376272 | tf_op jit(solution)/shard_map/reduce_scatter | solution.py:130
  (66 shorter events, 23.3 us)
Async XLA Ops:
  7.2 140.2 %copy-start = (bf16[5376,256]{1,0:T(8,128)(2,1)S(1)}, bf16[5376,256]{1,0:T(8,128)(2,1)}, u32[]{:S(2)}) copy-start(bf16[5376,256]{1,0:T(8,128)(2,1)} %param.16) | copy-start | bytes 8257540
  7.2 75.7 %reduce-scatter.12.cloned.1.call-start = ((), (), s32[]{:S(2)}) async-start(), calls=%async_computation.5 | async-start | bytes 1310720 | tf_op jit(solution)/shard_map/reduce_scatter | solution.py:121
  33.4 6.3 %slice-start = ((s8[5505024]{0:T(1024)(128)(4,1)}), s8[4194304]{0:T(1024)(128)(4,1)S(1)}, s32[]{:S(2)}) async-start(s8[5505024]{0:T(1024)(128)(4,1)} %bitcast.151), calls=%async_computation.11 | async-start | bytes 8388608
  35.7 4.1 slice-start.1
  38.2 8.6 %copy-start.2 = (f32[1536,512,2]{1,0,2:T(8,128)}, f32[1536,512,2]{1,0,2:T(8,128)S(1)}, u32[]{:S(2)}) copy-start(f32[1536,512,2]{1,0,2:T(8,128)S(1)} %get-tuple-element.31) | copy-start | bytes 18874372
  38.2 3.8 copy-start.8
  42.1 1.6 copy-start.6
  43.7 3.1 copy-start.10
  46.8 4.9 %copy-start.7 = (bf16[512,256]{1,0:T(8,128)(2,1)S(1)}, bf16[512,256]{1,0:T(8,128)(2,1)}, u32[]{:S(2)}) copy-start(bf16[512,256]{1,0:T(8,128)(2,1)} %param.11) | copy-start | bytes 786436
  50.1 1.7 copy-start.1
  54.0 54.8 %reduce-scatter.14.cloned.1.call-start = ((), (), s32[]{:S(2)}) async-start(), calls=%async_computation.6 | async-start | bytes 1310720 | tf_op jit(solution)/shard_map/reduce_scatter | solution.py:122
  59.5 148.8 %all-reduce.7.cloned.1.call-start = ((), (), s32[]{:S(2)}) async-start(), calls=%async_computation.10 | async-start | bytes 5505024
  89.0 25.1 %copy-start.3 = (bf16[2048,128]{1,0:T(8,128)(2,1)S(1)}, bf16[2048,128]{1,0:T(8,128)(2,1)}, u32[]{:S(2)}) copy-start(bf16[2048,128]{1,0:T(8,128)(2,1)} %all_gather.6) | copy-start | bytes 1572868
  113.5 172.4 %reduce-scatter.18.cloned.1.call-start = ((), (), s32[]{:S(2)}) async-start(), calls=%async_computation.8 | async-start | bytes 2924544
  122.7 4.9 %copy-start.9 = (bf16[128,2,512]{2,0,1:T(8,128)(2,1)S(1)}, bf16[128,2,512]{2,0,1:T(8,128)(2,1)}, u32[]{:S(2)}) copy-start(bf16[128,2,512]{2,0,1:T(8,128)(2,1)} %get-tuple-element.33) | copy-start | bytes 786436
  127.6 237.1 %reduce-scatter.20.cloned.1.call-start = ((), (), s32[]{:S(2)}) async-start(), calls=%async_computation.9 | async-start | bytes 2924544
  138.2 3.4 copy-start.5
  138.2 294.0 %reduce-scatter.16.cloned.1.call-start = ((), (), s32[]{:S(2)}) async-start(), calls=%async_computation.7 | async-start | bytes 12386304 | tf_op jit(solution)/shard_map/reduce_scatter | solution.py:130
  138.5 3.1 copy-start.4
  157.4 0.7 copy-start.11
Sparse Core Ops, SparseCore 0:
  54.2 28.6 reduce-scatter.11
  85.3 23.5 reduce-scatter.13
  113.6 94.6 all-reduce.6
  211.5 74.3 reduce-scatter.17
  289.1 75.6 reduce-scatter.19
  367.0 65.1 reduce-scatter.15
where the time goes:
time: 442 us; the launch traced here: 441 us
  waiting for transfers between devices  309 us (70%)
  matrix products  58.3 us (13%)
  blocking collectives  24.1 us (5%)
  local copies, waits for them, and re-layouts  22.5 us (5%)
  between operations  15 us (3%)
  other arithmetic  11.3 us (3%)
    unnamed x9, waiting for transfers between devices  201 us
    reduce_scatter x1, waiting for transfers between devices, on_device(): lax.psum_scatter(total, 'tensor', scatter_dimension=0, tiled=True)  65.5 us
    reduce_scatter x1, waiting for transfers between devices, on_device(): lax.psum_scatter(full_keys, 'context', scatter_dimension=0, tiled=True)  23.1 us
    dot_general x4, matrix products, contract_rows(): lax.dot_general(left, right, (((0,), (0,)), ((), ())), preferred_element_...  20.8 us
    unnamed x37, local copies, waits for them, and re-layouts  20.1 us
    reduce_scatter x1, waiting for transfers between devices, on_device(): lax.psum_scatter(full_values, 'context', scatter_dimension=0, tiled=True)  19.8 us
    dot_general x3, matrix products, contract_cols(): lax.dot_general(left, right, (((1,), (1,)), ((), ())), preferred_element_...  18.9 us
    all_gather x1, blocking collectives, on_device(): lax.all_gather(key_states, 'context', axis=0, tiled=True)  13.3 us
  transfers between devices with their start and end apart: 6, of which 6 were waited for; matrix products, arithmetic and copies ran while one was open for 14% of the time, Pallas kernels for 0%

commit v1 on v0

--- a/solution.py
+++ b/solution.py
@@ -59,7 +59,10 @@
     reach = min((W + count - 2) // count, blocks - 1)
     span = (reach + 1) * count
     whole_keys, whole_values = (
-        lax.all_gather(key_states, "context", axis=0, tiled=True),
+        jnp.concatenate(
+            lax.all_to_all(jnp.stack([key_states] * lax.axis_size("context")), "context", 0, 0),
+            axis=0,
+        ),
         lax.all_gather(value_states, "context", axis=0, tiled=True),
     )
     padding = jnp.zeros((reach * count, kv_cols), jnp.bfloat16)

time: 442 us -> 437 us (0.989)
  blocking collectives: 24.1 us -> 13.5 us
  starting transfers between devices: 0.65 us -> 5.61 us
    all_gather x1 -> x0, blocking collectives: 13.3 us -> none  [on_device(): lax.all_gather(key_states, 'context', axis=0, tiled=True)]
    all_to_all x0 -> x1, starting transfers between devices: none -> 5 us  [on_device(): lax.all_to_all(jnp.stack([key_states] * lax.axis_size('context')), 'conte...]
    unnamed x37 -> x33, local copies, waits for them, and re-layouts: 20.1 us -> 18 us
  transfers between devices with their start and end apart: 6 -> 7, of which waited for: 6 -> 6; matrix products, arithmetic and copies ran while one was open for 14% -> 16% of each run, Pallas kernels for 0% -> 0%
where the time goes in v1:
time: 437 us; the launch traced here: 436 us
  waiting for transfers between devices  307 us (70%)
  matrix products  62 us (14%)
  local copies, waits for them, and re-layouts  22.3 us (5%)
  between operations  15 us (3%)
  blocking collectives  13.5 us (3%)
  other arithmetic  10.4 us (2%)
  starting transfers between devices  5.61 us (1%)
    unnamed x9, waiting for transfers between devices  201 us
    reduce_scatter x1, waiting for transfers between devices, on_device(): lax.psum_scatter(total, 'tensor', scatter_dimension=0, tiled=True)  65.5 us
    reduce_scatter x1, waiting for transfers between devices, on_device(): lax.psum_scatter(full_keys, 'context', scatter_dimension=0, tiled=True)  20.9 us
    dot_general x4, matrix products, contract_rows(): lax.dot_general(left, right, (((0,), (0,)), ((), ())), preferred_element_...  20.7 us
    reduce_scatter x1, waiting for transfers between devices, on_device(): lax.psum_scatter(full_values, 'context', scatter_dimension=0, tiled=True)  19.8 us
    dot_general x3, matrix products, contract_cols(): lax.dot_general(left, right, (((1,), (1,)), ((), ())), preferred_element_...  18.9 us
    unnamed x33, local copies, waits for them, and re-layouts  18 us
    all_gather x1, blocking collectives, on_device(): lax.all_gather(value_states, 'context', axis=0, tiled=True)  13.5 us
  transfers between devices with their start and end apart: 7, of which 6 were waited for; matrix products, arithmetic and copies ran while one was open for 16% of the time, Pallas kernels for 0%

profile of v1, /device:TPU:1, one launch (start us, length us, event | category | flops | bytes accessed | tf_op | source)
XLA Modules:
  0.0 436.2 jit_solution(15270053207200182407)
XLA Ops:
  9.1 5.0 %all-to-all-start = ((bf16[4,512,128]{2,1,0:T(8,128)(2,1)}), bf16[4,512,128]{2,1,0:T(8,128)(2,1)}, u32[]{:S(2)}, u32[]{:S(2)}) async-start(bf16[4,512,128]{2,1,0:T(8,128)(2,1)} %stack.8), calls=%async_computation | async-start | bytes 1048576 | tf_op jit(solution)/shard_map/all_to_all | solution.py:63
  16.0 13.5 %all_gather.3 = bf16[2048,128]{1,0:T(8,128)(2,1)} all-gather(bf16[512,128]{1,0:T(8,128)(2,1)} %param.13), channel_id=1, replica_groups=mesh['dp'=4,'context'=4,'tensor'=8] {'context'}, dimensions={0}, use_global_device_ids=true | all-gather | bytes 655360 | tf_op jit(solution)/shard_map/all_gather | solution.py:66
  29.6 5.8 %convolution_convert_fusion.4 = bf16[512,256]{0,1:T(8,128)(2,1)} fusion(bf16[512,5376]{1,0:T(8,128)(2,1)} %param.14, bf16[5376,256]{1,0:T(8,128)(2,1)} %param.19), kind=kOutput, calls=%fused_computation.33 | convolution fusion | flops 1409417216 | bytes 8519680 | tf_op jit(solution)/shard_map/dot_general | solution.py:98
  36.8 2.5 fusion.9
  40.9 3.1 fusion.29
  44.0 3.2 fusion.10
  51.3 4.2 fusion.22
  56.9 20.9 %reduce-scatter.12.cloned.1.call-done = f32[512,128]{0,1:T(8,128)} async-done(((f32[2048,128]{0,1:T(8,128)}), f32[512,128]{0,1:T(8,128)}) %reduce-scatter.12.cloned.1.call-update) | async-done | bytes 262160 | tf_op jit(solution)/shard_map/reduce_scatter | solution.py:124
  79.3 4.6 %fusion.2 = bf16[5376,128]{0,1:T(8,128)(2,1)} fusion(bf16[512,128]{0,1:T(8,128)(2,1)S(1)} %bitcast.147, bf16[512,5376]{1,0:T(8,128)(2,1)} %param.10), kind=kOutput, calls=%fused_computation.7 | convolution fusion | flops 705331200 | bytes 7012352 | tf_op jit(solution)/shard_map/dot_general | solution.py:28
  83.9 19.8 %reduce-scatter.14.cloned.1.call-done = f32[512,128]{0,1:T(8,128)} async-done(((f32[2048,128]{0,1:T(8,128)}), f32[512,128]{0,1:T(8,128)}) %reduce-scatter.14.cloned.1.call-update) | async-done | bytes 262160 | tf_op jit(solution)/shard_map/reduce_scatter | solution.py:125
  103.7 4.7 %fusion.3 = bf16[5376,128]{0,1:T(8,128)(2,1)} fusion(bf16[512,5376]{1,0:T(8,128)(2,1)} %param.10, f32[512,128]{0,1:T(8,128)} %reduce-scatter.14.cloned.1.call-done), kind=kOutput, calls=%fused_computation.8 | convolution fusion | flops 705396736 | bytes 7143424 | tf_op jit(solution)/shard_map/dot_general | solution.py:28
  109.0 2.6 fusion.36
  111.7 5.7 %fusion = bf16[5376,256]{0,1:T(8,128)(2,1)} fusion(bf16[512,256]{0,1:T(8,128)(2,1)S(1)} %bitcast.149, bf16[512,5376]{1,0:T(8,128)(2,1)} %param.10), kind=kOutput, calls=%fused_computation.3 | convolution fusion | flops 1410662400 | bytes 8519680 | tf_op jit(solution)/shard_map/dot_general | solution.py:28
  117.4 4.9 %copy.64 = bf16[5376,256]{1,0:T(8,128)(2,1)} copy(bf16[5376,256]{0,1:T(8,128)(2,1)} %fusion) | data formatting | bytes 5505024
  122.4 5.8 %fusion.1 = bf16[5376,256]{0,1:T(8,128)(2,1)} fusion(bf16[512,256]{0,1:T(8,128)(2,1)S(1)} %bitcast.152, bf16[512,5376]{1,0:T(8,128)(2,1)} %param.14), kind=kOutput, calls=%fused_computation.4 | convolution fusion | flops 1410662400 | bytes 8519680 | tf_op jit(solution)/shard_map/dot_general | solution.py:28
  128.2 4.7 %copy.70 = bf16[5376,256]{1,0:T(8,128)(2,1)} copy(bf16[5376,256]{0,1:T(8,128)(2,1)} %fusion.1) | data formatting | bytes 5505024
  133.2 3.1 fusion.65
  136.3 5.8 %fusion.51 = f32[512,5376]{1,0:T(8,128)} fusion(bf16[5376,128]{1,0:T(8,128)(2,1)S(1)} %copy-done.3, f32[512,128]{0,1:T(8,128)S(1)} %copy-done.4), kind=kOutput, calls=%fused_computation.65 | convolution fusion | flops 704708608 | bytes 12648448 | tf_op jit(solution)/shard_map/dot_general | solution.py:34
  142.1 10.0 %add_add_fusion = f32[512,5376]{1,0:T(8,128)} fusion(f32[512,5376]{1,0:T(8,128)} %fusion.51, f32[512,5376]{1,0:T(8,128)S(1)} %fusion.65, bf16[512,256]{0,1:T(8,128)(2,1)S(1)} %bitcast.150, bf16[5376,256]{1,0:T(8,128)(2,1)S(1)} %copy-done), kind=kOutput, calls=%fused_computation | convolution fusion | flops 1414791168 | bytes 36044800 | tf_op jit(solution)/shard_map/dot_general | solution.py:34
  154.0 49.2 %all-reduce.7.cloned.1.call-done = (bf16[5376,128]{0,1:T(8,128)(2,1)}, bf16[5376,128]{0,1:T(8,128)(2,1)}) async-done(((bf16[5376,128]{0,1:T(8,128)(2,1)}, bf16[5376,128]{0,1:T(8,128)(2,1)}), (bf16[5376,128]{0,1:T(8,128)(2,1)}, bf16[5376,128]{0,1:T(8,128)(2,1)})) %all-reduce.7.cloned.1.call-update) | async-done | bytes 2752528
  205.9 74.9 %reduce-scatter.18.cloned.1.call-done = bf16[336,256]{1,0:T(8,128)(2,1)} async-done(((bf16[5376,256]{1,0:T(8,128)(2,1)}), bf16[336,256]{1,0:T(8,128)(2,1)}) %reduce-scatter.18.cloned.1.call-update) | async-done | bytes 172048
  282.7 76.9 %reduce-scatter.20.cloned.1.call-done = bf16[336,256]{1,0:T(8,128)(2,1)} async-done(((bf16[5376,256]{1,0:T(8,128)(2,1)}), bf16[336,256]{1,0:T(8,128)(2,1)}) %reduce-scatter.20.cloned.1.call-update) | async-done | bytes 172048
  361.6 65.5 %reduce-scatter.16.cloned.1.call-done = f32[64,5376]{1,0:T(8,128)} async-done(((f32[512,5376]{1,0:T(8,128)}), f32[64,5376]{1,0:T(8,128)}) %reduce-scatter.16.cloned.1.call-update) | async-done | bytes 1376272 | tf_op jit(solution)/shard_map/reduce_scatter | solution.py:133
  427.1 2.3 convert_element_type.102
  (63 shorter events, 22.8 us)
Async XLA Ops:
  7.2 135.0 %copy-start = (bf16[5376,256]{1,0:T(8,128)(2,1)S(1)}, bf16[5376,256]{1,0:T(8,128)(2,1)}, u32[]{:S(2)}) copy-start(bf16[5376,256]{1,0:T(8,128)(2,1)} %param.16) | copy-start | bytes 8257540
  9.1 27.7 %all-to-all-start = ((bf16[4,512,128]{2,1,0:T(8,128)(2,1)}), bf16[4,512,128]{2,1,0:T(8,128)(2,1)}, u32[]{:S(2)}, u32[]{:S(2)}) async-start(bf16[4,512,128]{2,1,0:T(8,128)(2,1)} %stack.8), calls=%async_computation | async-start | bytes 1048576 | tf_op jit(solution)/shard_map/all_to_all | solution.py:63
  14.1 63.7 %reduce-scatter.12.cloned.1.call-start = ((), (), s32[]{:S(2)}) async-start(), calls=%async_computation.6 | async-start | bytes 1310720 | tf_op jit(solution)/shard_map/reduce_scatter | solution.py:124
  29.6 5.8 %copy-start.7 = (s32[512]{0:T(512)S(1)}, s32[512]{0:T(512)}, u32[]{:S(2)}) copy-start(s32[512]{0:T(512)} %iota_add_fusion.1) | copy-start | bytes 6148
  29.6 5.8 %copy-start.8 = (s32[512]{0:T(512)S(1)}, s32[512]{0:T(512)}, u32[]{:S(2)}) copy-start(s32[512]{0:T(512)} %get-tuple-element.29) | copy-start | bytes 6148
  39.2 4.7 %copy-start.2 = (f32[1536,512,2]{1,0,2:T(8,128)}, f32[1536,512,2]{1,0,2:T(8,128)S(1)}, u32[]{:S(2)}) copy-start(f32[1536,512,2]{1,0,2:T(8,128)S(1)} %get-tuple-element.31) | copy-start | bytes 18874372
  39.3 1.5 copy-start.5
  39.3 1.7 copy-start.10
  44.0 4.9 %copy-start.6 = (bf16[512,256]{1,0:T(8,128)(2,1)S(1)}, bf16[512,256]{1,0:T(8,128)(2,1)}, u32[]{:S(2)}) copy-start(bf16[512,256]{1,0:T(8,128)(2,1)} %param.11) | copy-start | bytes 786436
  47.2 1.7 copy-start.1
  51.1 52.6 %reduce-scatter.14.cloned.1.call-start = ((), (), s32[]{:S(2)}) async-start(), calls=%async_computation.7 | async-start | bytes 1310720 | tf_op jit(solution)/shard_map/reduce_scatter | solution.py:125
  56.6 146.6 %all-reduce.7.cloned.1.call-start = ((), (), s32[]{:S(2)}) async-start(), calls=%async_computation.11 | async-start | bytes 5505024
  108.4 172.4 %reduce-scatter.18.cloned.1.call-start = ((), (), s32[]{:S(2)}) async-start(), calls=%async_computation.9 | async-start | bytes 2924544
  117.4 5.0 %copy-start.9 = (bf16[128,2,512]{2,0,1:T(8,128)(2,1)S(1)}, bf16[128,2,512]{2,0,1:T(8,128)(2,1)}, u32[]{:S(2)}) copy-start(bf16[128,2,512]{2,0,1:T(8,128)(2,1)} %get-tuple-element.33) | copy-start | bytes 786436
  122.3 237.3 %reduce-scatter.20.cloned.1.call-start = ((), (), s32[]{:S(2)}) async-start(), calls=%async_computation.10 | async-start | bytes 2924544
  132.9 3.4 copy-start.4
  132.9 294.2 %reduce-scatter.16.cloned.1.call-start = ((), (), s32[]{:S(2)}) async-start(), calls=%async_computation.8 | async-start | bytes 12386304 | tf_op jit(solution)/shard_map/reduce_scatter | solution.py:133
  133.2 3.1 copy-start.3
  152.1 0.7 copy-start.11
Sparse Core Ops, SparseCore 0:
  51.2 26.5 reduce-scatter.11
  80.2 23.4 reduce-scatter.13
  108.5 94.6 all-reduce.6
  206.4 74.3 reduce-scatter.17
  284.0 75.6 reduce-scatter.19
  361.9 65.1 reduce-scatter.15
